TPU v7x, 128 devices: a whole 4x4x4 slice. The times are simulated.
128 devices in a mesh: band: 8 (over z_hi, y), lon: 16 (over z_lo, x, core).
Axes of the slice: x: 4, y: 4, z: 4 (z_hi: 2, z_lo: 2; z = z_hi * 2 + z_lo), core: 2. Of those that a mesh axis runs over, the one named last changes fastest.
Arguments:
- latent: bfloat16 [256, 2048, 256], P('band', 'lon'), may hold values from -6 to 6
- row_index: int32 [8, 16, 32], P('band', 'lon'), may hold values from 0 to 31
- interp_weights: bfloat16 [4096, 128, 128], P(('band', 'lon')), may hold values from -0.5 to 0.5
- observation_slot_index: int32 [4096, 128], P(('band', 'lon')), may hold values from 0 to 6
- counts: int32 [4096], P(('band', 'lon')), may hold values from 32 to 128
- targets: bfloat16 [4096, 128, 128], P(('band', 'lon')), may hold values from -6 to 6
- gain: float32 [256], replicated, may hold values from 0.5 to 1.5
- w_in: bfloat16 [256, 512], replicated, may hold values from -0.375 to 0.375
- w_out: bfloat16 [512, 256], replicated, may hold values from -0.25 to 0.25
- head: bfloat16 [256, 128], replicated, may hold values from -0.375 to 0.375
Outputs:
- grad_latent: float32 [256, 2048, 256], P('band', 'lon')
- grad_w_in: float32 [256, 512], replicated
- grad_w_out: float32 [512, 256], replicated
- grad_gain: float32 [256], replicated
- grad_head: float32 [256, 128], replicated
All inputs are finite; a program needn't handle non-finite values.
Results may differ from a plain program's by a relative error of at most 0.007.
Values may be sent and summed in bfloat16 or wider, within the bound.
No kernel may reach another device: no remote copies, remote signals or barrier semaphores. Data moves between devices by JAX's collectives and lax.ppermute only.
A program may use at most 128 MiB of HBM per device.

v0:
```python
import math
import jax
import jax.numpy as jnp
from jax import lax
from jax.sharding import PartitionSpec as P

WINDOW_SLOTS = 7
norm_eps = 1e-05


def padded_2(cells, sides, width):
    for axis, dim in sides:
        count = lax.axis_size(axis)
        head = lax.slice_in_dim(cells, 0, width, axis=dim)
        tail = lax.slice_in_dim(cells, cells.shape[dim] - width, cells.shape[dim], axis=dim)
        cells = jnp.concatenate(
            [
                lax.ppermute(tail, axis, [(i, (i + 1) % count) for i in range(count)]),
                cells,
                lax.ppermute(head, axis, [((i + 1) % count, i) for i in range(count)]),
            ],
            axis=dim,
        )
    return cells


def rounded_slots(values):
    return lax.optimization_barrier(values.astype(jnp.bfloat16))


def padded_mix(padded):
    return padded[:, 1:-1] + 0.5 * (padded[:, :-2] + padded[:, 2:])


def silu_slope(pre_act):
    sigmoid_a = jax.nn.sigmoid(pre_act)
    return sigmoid_a * (1.0 + pre_act * (1.0 - sigmoid_a))


def project_pair(weights, tile_pairs, temporal_weight, channels):
    proj_old = jnp.einsum(
        "bol,blc->boc", weights, tile_pairs[..., :channels], preferred_element_type=jnp.float32
    )
    proj_new = jnp.einsum(
        "bol,blc->boc", weights, tile_pairs[..., channels:], preferred_element_type=jnp.float32
    )
    return ((1.0 - temporal_weight) * proj_old + temporal_weight * proj_new).astype(jnp.bfloat16)


def pull_back(weights, obs_grad, temporal_weight):
    obs_float = obs_grad.astype(jnp.float32)
    back_old = ((1.0 - temporal_weight) * obs_float).astype(jnp.bfloat16)
    back_new = (temporal_weight * obs_float).astype(jnp.bfloat16)
    tile_old = jnp.einsum("bol,boc->blc", weights, back_old, preferred_element_type=jnp.float32)
    tile_new = jnp.einsum("bol,boc->blc", weights, back_new, preferred_element_type=jnp.float32)
    return jnp.concatenate([tile_old, tile_new], axis=-1).astype(jnp.bfloat16)


def decode(obs_latent, live_rows, goals, head, loss_scale):
    blocks, obs_rows, channels = obs_latent.shape
    flat_latent = obs_latent.reshape(-1, channels)
    predicted = jnp.dot(flat_latent, head, preferred_element_type=jnp.float32)
    residual = jnp.where(
        live_rows, predicted - goals.reshape(-1, head.shape[1]).astype(jnp.float32), 0.0
    )
    pred_grad = (residual * loss_scale).astype(jnp.bfloat16)
    head_grad = jnp.einsum("rc,rv->cv", flat_latent, pred_grad, preferred_element_type=jnp.float32)
    obs_grad = jnp.einsum("rv,cv->rc", pred_grad, head, preferred_element_type=jnp.float32).astype(
        jnp.bfloat16
    )
    return (head_grad, obs_grad.reshape(blocks, obs_rows, channels))


def body(
    latent,
    row_index,
    interp_weights,
    observation_slot_index,
    counts,
    targets,
    gain,
    w_in,
    w_out,
    head,
):
    lat_rows, lon_cells, channels = latent.shape
    peer_count = lax.axis_size("lon")
    devices_all = lax.axis_size("band") * peer_count
    blocks = interp_weights.shape[0]
    obs_rows = interp_weights.shape[1]
    per_peer = blocks // peer_count
    padded = padded_2(latent, (("lon", 1),), 1)
    summed = padded_mix(padded.astype(jnp.float32))
    inv_rms = lax.rsqrt(jnp.mean(summed * summed, axis=-1, keepdims=True) + norm_eps)
    normed = (summed * inv_rms * gain).astype(jnp.bfloat16)
    pre_act = jnp.einsum("lmc,ch->lmh", normed, w_in, preferred_element_type=jnp.float32)
    activated = jax.nn.silu(pre_act).astype(jnp.bfloat16)
    advanced = (
        latent.astype(jnp.float32)
        + jnp.einsum("lmh,hc->lmc", activated, w_out, preferred_element_type=jnp.float32)
    ).astype(jnp.bfloat16)
    stacked = jnp.concatenate([latent, advanced], axis=-1)
    requested = row_index.reshape(blocks)
    picked = stacked[requested]
    row_select = (requested[:, None] == jnp.arange(lat_rows, dtype=jnp.int32)[None, :]).astype(
        jnp.bfloat16
    )
    temporal_weight = rounded_slots(observation_slot_index.astype(jnp.float32) / (WINDOW_SLOTS - 1))
    live_flags = jnp.arange(obs_rows, dtype=jnp.int32)[None, :] < counts[:, None]
    live_rows = live_flags.reshape(-1, 1)
    loss_scale = 1.0 / math.sqrt(obs_rows)
    tile_pairs = lax.all_to_all(
        picked.reshape(peer_count, per_peer, lon_cells, 2 * channels),
        "lon",
        split_axis=0,
        concat_axis=0,
        tiled=True,
    )
    local_coef = temporal_weight.reshape(blocks, obs_rows, 1).astype(jnp.float32)
    obs_latent = project_pair(
        interp_weights, tile_pairs.reshape(blocks, lon_cells, 2 * channels), local_coef, channels
    )
    head_grad, obs_grad = decode(obs_latent, live_rows, targets, head, loss_scale)
    tile_grads = pull_back(interp_weights, obs_grad, local_coef)
    returned = lax.all_to_all(
        tile_grads.reshape(peer_count, per_peer, lon_cells, 2 * channels),
        "lon",
        split_axis=0,
        concat_axis=0,
        tiled=True,
    )
    grid_grad = jnp.einsum(
        "br,bx->rx",
        row_select,
        returned.reshape(blocks, lon_cells * 2 * channels),
        preferred_element_type=jnp.float32,
    )
    grid_grad = grid_grad.reshape(lat_rows, lon_cells, 2 * channels)
    grad_adv = grid_grad[..., channels:].astype(jnp.bfloat16)
    grad_out = jnp.einsum("lmh,lmc->hc", activated, grad_adv, preferred_element_type=jnp.float32)
    act_grad = jnp.einsum("lmc,hc->lmh", grad_adv, w_out, preferred_element_type=jnp.float32)
    pre_grad = (act_grad * silu_slope(pre_act)).astype(jnp.bfloat16)
    grad_in = jnp.einsum("lmc,lmh->ch", normed, pre_grad, preferred_element_type=jnp.float32)
    normed_grad = jnp.einsum("lmh,ch->lmc", pre_grad, w_in, preferred_element_type=jnp.float32)
    grad_gain = jnp.sum(normed_grad * summed * inv_rms, axis=(0, 1))
    gained = normed_grad * gain
    summed_grad = inv_rms * (
        gained - summed * inv_rms * inv_rms * jnp.mean(gained * summed, axis=-1, keepdims=True)
    )
    grad_padded = padded_2(summed_grad.astype(jnp.bfloat16), (("lon", 1),), 1).astype(
        summed_grad.dtype
    )
    grad_latent = grid_grad[..., :channels] + grid_grad[..., channels:] + padded_mix(grad_padded)
    totals = lax.psum((grad_in, grad_out, grad_gain, head_grad), ("band", "lon"))
    return (
        grad_latent,
        totals[0] / devices_all,
        totals[1] / devices_all,
        totals[2] / devices_all,
        totals[3] / devices_all,
    )


def solution(mesh):
    return jax.shard_map(
        body,
        mesh=mesh,
        in_specs=(
            P("band", "lon", None),
            P("band", "lon", None),
            P(("band", "lon"), None, None),
            P(("band", "lon"), None),
            P(("band", "lon")),
            P(("band", "lon"), None, None),
            P(),
            P(),
            P(),
            P(),
        ),
        out_specs=(P("band", "lon", None), P(), P(), P(), P()),
        check_vma=False,
    )
```

profile of v0, /device:TPU:1, one launch (start us, length us, event | category | flops | bytes accessed | tf_op | source)
XLA Modules:
  0.0 456.2 jit_solution(16606701495915434797)
XLA Ops:
  7.2 0.0 copy-start
  7.2 2.9 copy.28
  10.1 2.7 collective-permute-start
  12.7 0.0 collective-permute-start.1
  12.8 0.8 collective-permute-done
  13.6 2.6 collective-permute-done.1
  16.2 0.3 maximum_convert_fusion
  16.5 0.0 copy-start.17
  16.5 0.8 multiply_reduce_fusion.2
  17.4 0.0 copy-start.4
  17.4 0.0 copy-start.21
  17.4 0.8 multiply_convert_fusion.5
  18.2 0.3 copy-done.21
  18.5 5.2 %multiply_convert_fusion.1 = (bf16[32,128,512]{2,1,0:T(8,128)(2,1)S(1)}, f32[32,128,512]{2,1,0:T(8,128)}) fusion(bf16[256,512]{1,0:T(8,128)(2,1)S(1)} %copy-done.21, bf16[32,128,256]{2,0,1:T(8,128)(2,1)S(1)} %multiply_convert_fusion.5), kind=kOutput, calls=%fused_computation.2 | convolution fusion | flops 1084227584 | bytes 14942208 | tf_op jit(solution)/shard_map/lmc,ch->lmh/dot_general | solution.py:96
  23.7 1.9 copy-done.10
  25.6 1.3 add_convert_fusion.1
  26.9 2.3 pad_maximum_fusion
  29.2 5.0 %gather_fusion = bf16[32,128,512]{2,1,0:T(8,128)(2,1)} fusion(bf16[32,128,512]{2,1,0:T(8,128)(2,1)} %pad_maximum_fusion, s32[1024]{0:T(1024)S(1)} %pad_clamp_fusion), kind=kCustom, calls=%fused_computation | custom fusion | bytes 8388736 | tf_op jit(solution)/shard_map/gather | solution.py:104
  34.2 6.4 %all-to-all-start = ((bf16[16,2,128,512]{3,2,1,0:T(8,128)(2,1)}), bf16[16,2,128,512]{3,2,1,0:T(8,128)(2,1)}, u32[]{:S(2)}, u32[]{:S(2)}) async-start(bf16[16,2,128,512]{3,2,1,0:T(8,128)(2,1)} %bitcast.68), calls=%async_computation | async-start | bytes 8388608 | tf_op jit(solution)/shard_map/all_to_all | solution.py:112
  40.7 0.1 fusion.41
  40.8 56.3 %all-to-all-done = bf16[16,2,128,512]{3,2,1,0:T(8,128)(2,1)} async-done(((bf16[16,2,128,512]{3,2,1,0:T(8,128)(2,1)}), bf16[16,2,128,512]{3,2,1,0:T(8,128)(2,1)}, u32[]{:S(2)}, u32[]{:S(2)}) %all-to-all-start) | async-done | bytes 4194336 | tf_op jit(solution)/shard_map/all_to_all | solution.py:112
  97.0 2.3 fusion.18
  99.3 0.0 copy-start.15
  99.3 0.0 copy-start.20
  99.4 2.6 add_convert_fusion
  102.0 1.4 copy-done.6
  103.4 2.3 fusion.2
  105.7 1.1 copy-done.8
  106.7 0.7 convolution_convert_fusion
  107.4 3.4 copy.32
  110.9 3.0 fusion.24
  113.9 0.4 copy-done.3
  114.3 2.0 fusion.25
  116.3 3.9 copy.34
  120.3 2.6 copy.35
  122.8 4.6 %pad_maximum_fusion.1 = bf16[16,2,128,512]{3,2,1,0:T(8,128)(2,1)} fusion(bf16[16,2,128,256]{3,2,1,0:T(8,128)(2,1)} %copy.35, bf16[16,2,128,256]{3,2,1,0:T(8,128)(2,1)} %copy.34), kind=kLoop, calls=%fused_computation.21 | loop fusion | flops 8388608 | bytes 8388608 | tf_op jit(solution)/shard_map/concatenate | solution.py:56
  127.5 5.1 %all-to-all-start.1 = ((bf16[16,2,128,512]{3,2,1,0:T(8,128)(2,1)}), bf16[16,2,128,512]{3,2,1,0:T(8,128)(2,1)}, u32[]{:S(2)}, u32[]{:S(2)}) async-start(bf16[16,2,128,512]{3,2,1,0:T(8,128)(2,1)} %pad_maximum_fusion.1), calls=%async_computation.1 | async-start | bytes 8388608 | tf_op jit(solution)/shard_map/all_to_all | solution.py:125
  132.6 0.3 all-reduce.3.cloned.1.call-start
  132.9 1.4 fusion.47
  134.3 54.1 %all-to-all-done.1 = bf16[16,2,128,512]{3,2,1,0:T(8,128)(2,1)} async-done(((bf16[16,2,128,512]{3,2,1,0:T(8,128)(2,1)}), bf16[16,2,128,512]{3,2,1,0:T(8,128)(2,1)}, u32[]{:S(2)}, u32[]{:S(2)}) %all-to-all-start.1) | async-done | bytes 4194336 | tf_op jit(solution)/shard_map/all_to_all | solution.py:125
  188.4 5.4 %fusion.3 = f32[32,128,512]{2,0,1:T(8,128)S(1)} fusion(s32[32]{0:T(128)S(1)} %bitcast.74, bf16[4,8,128,512]{3,2,1,0:T(8,128)(2,1)} %bitcast.28), kind=kOutput, calls=%fused_computation.9 | convolution fusion | flops 134218752 | bytes 12583040 | tf_op jit(solution)/shard_map/br,bx->rx/dot_general | solution.py:132
  193.8 0.3 slice.98
  194.2 4.9 %copy-done.11 = bf16[32,128,512]{2,1,0:T(8,128)(2,1)S(1)} copy-done((bf16[32,128,512]{2,1,0:T(8,128)(2,1)S(1)}, bf16[32,128,512]{2,1,0:T(8,128)(2,1)}, u32[]{:S(2)}) %copy-start.11) | copy-done | bytes 4194328
  199.1 3.6 fusion.32
  202.6 6.6 %multiply_convert_fusion = bf16[32,128,512]{2,1,0:T(8,128)(2,1)S(1)} fusion(f32[32,128,512]{2,1,0:T(8,128)} %get-tuple-element.27, bf16[32,128,256]{2,0,1:T(8,128)(2,1)S(1)} %slice.98, bf16[512,256]{1,0:T(8,128)(2,1)S(1)} %copy-done.14), kind=kOutput, calls=%fused_computation.1 | convolution fusion | flops 1092616192 | bytes 14942208 | tf_op jit(solution)/shard_map/lmc,hc->lmh/dot_general | solution.py:141
  209.2 1.9 copy-done.23
  211.2 3.7 fusion.29
  214.8 8.9 %multiply_reduce_fusion = (f32[256]{0:T(256)S(1)}, f32[32,128]{0,1:T(8,128)S(1)}, f32[32,128,256]{2,0,1:T(8,128)}) fusion(f32[32,128,256]{2,0,1:T(8,128)} %copy-done.4, f32[32,128]{0,1:T(8,128)S(1)} %add_rsqrt_fusion, f32[256]{0:T(256)S(1)} %copy-done.17, bf16[256,512]{1,0:T(8,128)(2,1)S(1)} %copy-done.22, bf16[32,128,512]{2,1,0:T(8,128)(2,1)} %copy-done.23), kind=kOutput, calls=%fused_computation.22 | convolution fusion | flops 1080028928 | bytes 12879872 | tf_op jit(solution)/shard_map/lmh,ch->lmc/dot_general | solution.py:144
  223.7 67.3 %psum.30 = f32[256]{0:T(256)S(1)} all-reduce(f32[256]{0:T(256)S(1)} %get-tuple-element.15), channel_id=1, replica_groups=mesh['band'=8,'lon'=16] {'band','lon'}, use_global_device_ids=true, to_apply=%region_5.6 | all-reduce | flops 256 | bytes 2048 | tf_op jit(solution)/shard_map/psum | solution.py:154
  291.1 4.1 multiply_convert_fusion.2
  295.2 0.7 collective-permute-start.2
  295.9 0.5 collective-permute-start.3
  296.4 0.6 broadcast_multiply_fusion.4
  297.0 0.0 all-reduce.3.cloned.1.call-update
  297.0 0.0 collective-permute-done.2
  297.0 2.0 collective-permute-done.3
  299.1 0.3 maximum_convert_fusion.1
  299.4 0.0 copy-start.1
  299.4 5.1 %fusion.8 = f32[32,128,256]{2,0,1:T(8,128)S(1)} fusion(f32[32,130,256]{2,0,1:T(8,128)S(1)} %maximum_convert_fusion.1, f32[32,128,512]{2,0,1:T(8,128)} %copy-done.2), kind=kLoop, calls=%fused_computation.15 | loop fusion | flops 5242880 | bytes 25165824 | tf_op jit(solution)/shard_map/add | solution.py:153
  304.5 4.4 copy.43
  309.0 135.1 %all-reduce.3.cloned.1.call-done = (f32[256,512]{1,0:T(8,128)}, f32[512,256]{1,0:T(8,128)}, f32[256,128]{1,0:T(8,128)}) async-done(((f32[256,512]{1,0:T(8,128)}, f32[512,256]{1,0:T(8,128)}, f32[256,128]{1,0:T(8,128)}), (f32[256,512]{1,0:T(8,128)}, f32[512,256]{1,0:T(8,128)}, f32[256,128]{1,0:T(8,128)})) %all-reduce.3.cloned.1.call-update) | async-done | bytes 1179664 | tf_op jit(solution)/shard_map/psum | solution.py:154
  444.1 1.9 broadcast_multiply_fusion.1
  445.9 1.6 broadcast_multiply_fusion.2
  447.5 1.9 broadcast_multiply_fusion
  (43 shorter events, 0.1 us)
Async XLA Ops:
  7.2 89.9 %copy-start = (bf16[32,128,128]{2,1,0:T(8,128)(2,1)S(1)}, bf16[32,128,128]{2,1,0:T(8,128)(2,1)}, u32[]{:S(2)}) copy-start(bf16[32,128,128]{2,1,0:T(8,128)(2,1)} %param.12) | copy-start | bytes 3145732
  7.2 5.6 %copy-start.18 = (s32[1,1,32]{2,1,0:T(1,128)S(1)}, s32[1,1,32]{2,1,0:T(1,128)}, u32[]{:S(2)}) copy-start(s32[1,1,32]{2,1,0:T(1,128)} %param.11) | copy-start | bytes 388
  10.1 3.5 collective-permute-start
  12.7 3.5 collective-permute-start.1
  16.5 0.9 copy-start.17
  17.4 6.3 %copy-start.4 = (f32[32,128,256]{2,0,1:T(8,128)}, f32[32,128,256]{2,0,1:T(8,128)S(1)}, u32[]{:S(2)}) copy-start(f32[32,128,256]{2,0,1:T(8,128)S(1)} %get-tuple-element.21) | copy-start | bytes 12582916
  17.4 1.1 copy-start.21
  18.5 5.2 %copy-start.12 = (bf16[32,128,256]{2,0,1:T(8,128)(2,1)}, bf16[32,128,256]{2,0,1:T(8,128)(2,1)S(1)}, u32[]{:S(2)}) copy-start(bf16[32,128,256]{2,0,1:T(8,128)(2,1)S(1)} %multiply_convert_fusion.5) | copy-start | bytes 6291460
  18.5 7.1 %copy-start.5 = (bf16[32,128,256]{2,1,0:T(8,128)(2,1)S(1)}, bf16[32,128,256]{2,1,0:T(8,128)(2,1)}, u32[]{:S(2)}) copy-start(bf16[32,128,256]{2,1,0:T(8,128)(2,1)} %param.10) | copy-start | bytes 6291460
  18.5 7.1 %copy-start.14 = (bf16[512,256]{1,0:T(8,128)(2,1)S(1)}, bf16[512,256]{1,0:T(8,128)(2,1)}, u32[]{:S(2)}) copy-start(bf16[512,256]{1,0:T(8,128)(2,1)} %param.18) | copy-start | bytes 786436
  23.7 1.9 copy-start.10
  34.2 6.5 %copy-start.16 = (s32[32,128]{1,0:T(8,128)S(1)}, s32[32,128]{1,0:T(8,128)}, u32[]{:S(2)}) copy-start(s32[32,128]{1,0:T(8,128)} %param.13) | copy-start | bytes 49156
  34.2 6.5 %copy-start.19 = (s32[32]{0:T(128)S(1)}, s32[32]{0:T(128)}, u32[]{:S(2)}) copy-start(s32[32]{0:T(128)} %param.14) | copy-start | bytes 388
  34.2 62.8 %all-to-all-start = ((bf16[16,2,128,512]{3,2,1,0:T(8,128)(2,1)}), bf16[16,2,128,512]{3,2,1,0:T(8,128)(2,1)}, u32[]{:S(2)}, u32[]{:S(2)}) async-start(bf16[16,2,128,512]{3,2,1,0:T(8,128)(2,1)} %bitcast.68), calls=%async_computation | async-start | bytes 8388608 | tf_op jit(solution)/shard_map/all_to_all | solution.py:112
  99.3 4.1 copy-start.15
  99.3 4.1 copy-start.20
  102.0 1.4 copy-start.6
  105.7 1.1 copy-start.8
  110.9 3.4 copy-start.3
  127.5 5.4 %copy-start.7 = (bf16[32,256,128]{1,2,0:T(8,128)(2,1)S(1)}, bf16[32,256,128]{1,2,0:T(8,128)(2,1)}, u32[]{:S(2)}) copy-start(bf16[32,256,128]{1,2,0:T(8,128)(2,1)} %copy-done.6) | copy-start | bytes 6291460
  127.5 5.4 %copy-start.9 = (bf16[4096,128]{1,0:T(8,128)(2,1)S(1)}, bf16[4096,128]{1,0:T(8,128)(2,1)}, u32[]{:S(2)}) copy-start(bf16[4096,128]{1,0:T(8,128)(2,1)} %copy-done.8) | copy-start | bytes 3145732
  127.5 60.9 %all-to-all-start.1 = ((bf16[16,2,128,512]{3,2,1,0:T(8,128)(2,1)}), bf16[16,2,128,512]{3,2,1,0:T(8,128)(2,1)}, u32[]{:S(2)}, u32[]{:S(2)}) async-start(bf16[16,2,128,512]{3,2,1,0:T(8,128)(2,1)} %pad_maximum_fusion.1), calls=%async_computation.1 | async-start | bytes 8388608 | tf_op jit(solution)/shard_map/all_to_all | solution.py:125
  132.6 311.5 %all-reduce.3.cloned.1.call-start = ((), (), s32[]{:S(2)}) async-start(), calls=%async_computation.2 | async-start | bytes 2359296 | tf_op jit(solution)/shard_map/psum | solution.py:154
  193.8 8.8 %copy-start.2 = (f32[32,128,512]{2,0,1:T(8,128)}, f32[32,128,512]{2,0,1:T(8,128)S(1)}, u32[]{:S(2)}) copy-start(f32[32,128,512]{2,0,1:T(8,128)S(1)} %fusion.3) | copy-start | bytes 25165828
  193.8 5.2 %copy-start.11 = (bf16[32,128,512]{2,1,0:T(8,128)(2,1)S(1)}, bf16[32,128,512]{2,1,0:T(8,128)(2,1)}, u32[]{:S(2)}) copy-start(bf16[32,128,512]{2,1,0:T(8,128)(2,1)} %copy-done.10) | copy-start | bytes 12582916
  202.6 8.5 %copy-start.13 = (bf16[32,128,256]{2,0,1:T(8,128)(2,1)S(1)}, bf16[32,128,256]{2,0,1:T(8,128)(2,1)}, u32[]{:S(2)}) copy-start(bf16[32,128,256]{2,0,1:T(8,128)(2,1)} %copy-done.12) | copy-start | bytes 6291460
  209.2 2.0 copy-start.23
  211.1 3.7 copy-start.22
  295.2 1.8 collective-permute-start.2
  295.9 3.2 collective-permute-start.3
  299.4 150.0 %copy-start.1 = (bf16[32,128,128]{2,1,0:T(8,128)(2,1)S(1)}, bf16[32,128,128]{2,1,0:T(8,128)(2,1)}, u32[]{:S(2)}) copy-start(bf16[32,128,128]{2,1,0:T(8,128)(2,1)} %param.12) | copy-start | bytes 3145732
Sparse Core Ops, SparseCore 0:
  297.2 146.8 all-reduce.2
where the time goes:
time: 457 us; the launch traced here: 456 us
  waiting for transfers between devices  251 us (55%)
  blocking collectives  67.3 us (15%)
  matrix products  48.9 us (11%)
  local copies, waits for them, and re-layouts  34.6 us (8%)
  other arithmetic  24.4 us (5%)
  starting transfers between devices  15.7 us (3%)
  between operations  14.3 us (3%)
    psum x1, waiting for transfers between devices, body(): lax.psum((grad_in, grad_out, grad_gain, head_grad), ('band', 'lon'))  135 us
    psum x1, blocking collectives, body(): lax.psum((grad_in, grad_out, grad_gain, head_grad), ('band', 'lon'))  67.3 us
    all_to_all x1, waiting for transfers between devices, body(): lax.all_to_all(picked.reshape(peer_count, per_peer, lon_cells, 2 * channe...  56.3 us
    all_to_all x1, waiting for transfers between devices, body(): lax.all_to_all(tile_grads.reshape(peer_count, per_peer, lon_cells, 2 * ch...  54.1 us
    unnamed x50, local copies, waits for them, and re-layouts  19.3 us
  transfers between devices with their start and end apart: 7, of which 6 were waited for; matrix products, arithmetic and copies ran while one was open for 3% of the time, Pallas kernels for 0%

commit v1 on v0

--- a/solution.py
+++ b/solution.py
@@ -151,7 +151,9 @@
         summed_grad.dtype
     )
     grad_latent = grid_grad[..., :channels] + grid_grad[..., channels:] + padded_mix(grad_padded)
-    totals = lax.psum((grad_in, grad_out, grad_gain, head_grad), ("band", "lon"))
+    totals = (grad_in, grad_out, grad_gain, head_grad)
+    for mesh_axis in ("lon", "band"):
+        totals = lax.psum(totals, mesh_axis)
     return (
         grad_latent,
         totals[0] / devices_all,

time: 457 us -> 441 us (0.965)
  blocking collectives: 67.3 us -> 50.8 us
    psum x1 -> x2, blocking collectives: 67.3 us -> 50.8 us  [body(): totals = lax.psum(totals, mesh_axis)]
    psum x1 -> x2, waiting for transfers between devices: 135 us -> 138 us  [body(): totals = lax.psum(totals, mesh_axis)]
    unnamed x50 -> x52, local copies, waits for them, and re-layouts: 19.3 us -> 19.3 us
  transfers between devices with their start and end apart: 7 -> 8, of which waited for: 6 -> 6; matrix products, arithmetic and copies ran while one was open for 3% -> 5% of each run, Pallas kernels for 0% -> 0%
where the time goes in v1:
time: 441 us; the launch traced here: 437 us
  waiting for transfers between devices  252 us (57%)
  blocking collectives  50.8 us (12%)
  matrix products  47.2 us (11%)
  local copies, waits for them, and re-layouts  34.6 us (8%)
  other arithmetic  21.7 us (5%)
  starting transfers between devices  15.9 us (4%)
  between operations  14.4 us (3%)
    psum x2, waiting for transfers between devices, body(): totals = lax.psum(totals, mesh_axis)  138 us
    all_to_all x1, waiting for transfers between devices, body(): lax.all_to_all(picked.reshape(peer_count, per_peer, lon_cells, 2 * channe...  56.3 us
    all_to_all x1, waiting for transfers between devices, body(): lax.all_to_all(tile_grads.reshape(peer_count, per_peer, lon_cells, 2 * ch...  54.1 us
    psum x2, blocking collectives, body(): totals = lax.psum(totals, mesh_axis)  50.8 us
    unnamed x52, local copies, waits for them, and re-layouts  19.3 us
  transfers between devices with their start and end apart: 8, of which 6 were waited for; matrix products, arithmetic and copies ran while one was open for 5% of the time, Pallas kernels for 0%

profile of v1, /device:TPU:1, one launch (start us, length us, event | category | flops | bytes accessed | tf_op | source)
XLA Modules:
  0.0 436.7 jit_solution(12731923982803242846)
XLA Ops:
  7.2 0.0 copy-start
  7.2 2.9 copy.28
  10.1 2.7 collective-permute-start
  12.8 0.8 collective-permute-done
  13.6 2.6 collective-permute-done.1
  16.2 0.3 maximum_convert_fusion
  16.5 0.0 copy-start.18
  16.5 0.8 multiply_reduce_fusion.2
  17.4 0.0 copy-start.4
  17.4 0.0 copy-start.22
  17.4 0.8 multiply_convert_fusion.5
  18.2 0.3 copy-done.22
  18.5 5.2 %multiply_convert_fusion.1 = (bf16[32,128,512]{2,1,0:T(8,128)(2,1)S(1)}, f32[32,128,512]{2,1,0:T(8,128)}) fusion(bf16[256,512]{1,0:T(8,128)(2,1)S(1)} %copy-done.22, bf16[32,128,256]{2,0,1:T(8,128)(2,1)S(1)} %multiply_convert_fusion.5), kind=kOutput, calls=%fused_computation.2 | convolution fusion | flops 1084227584 | bytes 14942208 | tf_op jit(solution)/shard_map/lmc,ch->lmh/dot_general | solution.py:96
  23.7 1.9 copy-done.11
  25.6 1.3 add_convert_fusion.1
  26.9 2.3 pad_maximum_fusion
  29.2 5.0 %gather_fusion = bf16[32,128,512]{2,1,0:T(8,128)(2,1)} fusion(bf16[32,128,512]{2,1,0:T(8,128)(2,1)} %pad_maximum_fusion, s32[1024]{0:T(1024)S(1)} %pad_clamp_fusion), kind=kCustom, calls=%fused_computation | custom fusion | bytes 8388736 | tf_op jit(solution)/shard_map/gather | solution.py:104
  34.2 6.4 %all-to-all-start = ((bf16[16,2,128,512]{3,2,1,0:T(8,128)(2,1)}), bf16[16,2,128,512]{3,2,1,0:T(8,128)(2,1)}, u32[]{:S(2)}, u32[]{:S(2)}) async-start(bf16[16,2,128,512]{3,2,1,0:T(8,128)(2,1)} %bitcast.68), calls=%async_computation | async-start | bytes 8388608 | tf_op jit(solution)/shard_map/all_to_all | solution.py:112
  40.7 0.1 fusion.41
  40.8 56.3 %all-to-all-done = bf16[16,2,128,512]{3,2,1,0:T(8,128)(2,1)} async-done(((bf16[16,2,128,512]{3,2,1,0:T(8,128)(2,1)}), bf16[16,2,128,512]{3,2,1,0:T(8,128)(2,1)}, u32[]{:S(2)}, u32[]{:S(2)}) %all-to-all-start) | async-done | bytes 4194336 | tf_op jit(solution)/shard_map/all_to_all | solution.py:112
  97.0 2.3 fusion.18
  99.3 0.0 copy-start.21
  99.4 2.6 add_convert_fusion
  102.0 1.4 copy-done.7
  103.4 2.3 fusion.2
  105.7 1.1 copy-done.9
  106.7 0.7 convolution_convert_fusion
  107.4 3.4 copy.32
  110.9 3.0 fusion.24
  113.9 0.4 copy-done.3
  114.3 2.0 fusion.25
  116.3 3.9 copy.34
  120.3 2.6 copy.35
  122.8 4.6 %pad_maximum_fusion.1 = bf16[16,2,128,512]{3,2,1,0:T(8,128)(2,1)} fusion(bf16[16,2,128,256]{3,2,1,0:T(8,128)(2,1)} %copy.35, bf16[16,2,128,256]{3,2,1,0:T(8,128)(2,1)} %copy.34), kind=kLoop, calls=%fused_computation.21 | loop fusion | flops 8388608 | bytes 8388608 | tf_op jit(solution)/shard_map/concatenate | solution.py:56
  127.5 5.1 %all-to-all-start.1 = ((bf16[16,2,128,512]{3,2,1,0:T(8,128)(2,1)}), bf16[16,2,128,512]{3,2,1,0:T(8,128)(2,1)}, u32[]{:S(2)}, u32[]{:S(2)}) async-start(bf16[16,2,128,512]{3,2,1,0:T(8,128)(2,1)} %pad_maximum_fusion.1), calls=%async_computation.1 | async-start | bytes 8388608 | tf_op jit(solution)/shard_map/all_to_all | solution.py:125
  132.6 0.3 all-reduce.5.cloned.1.call-start
  132.9 1.4 fusion.47
  134.3 54.1 %all-to-all-done.1 = bf16[16,2,128,512]{3,2,1,0:T(8,128)(2,1)} async-done(((bf16[16,2,128,512]{3,2,1,0:T(8,128)(2,1)}), bf16[16,2,128,512]{3,2,1,0:T(8,128)(2,1)}, u32[]{:S(2)}, u32[]{:S(2)}) %all-to-all-start.1) | async-done | bytes 4194336 | tf_op jit(solution)/shard_map/all_to_all | solution.py:125
  188.4 5.4 %fusion.3 = f32[32,128,512]{2,0,1:T(8,128)S(1)} fusion(s32[32]{0:T(128)S(1)} %bitcast.74, bf16[4,8,128,512]{3,2,1,0:T(8,128)(2,1)} %bitcast.28), kind=kOutput, calls=%fused_computation.9 | convolution fusion | flops 134218752 | bytes 12583040 | tf_op jit(solution)/shard_map/br,bx->rx/dot_general | solution.py:132
  193.8 0.3 slice.98
  194.2 4.9 %copy-done.12 = bf16[32,128,512]{2,1,0:T(8,128)(2,1)S(1)} copy-done((bf16[32,128,512]{2,1,0:T(8,128)(2,1)S(1)}, bf16[32,128,512]{2,1,0:T(8,128)(2,1)}, u32[]{:S(2)}) %copy-start.12) | copy-done | bytes 4194328
  199.1 3.6 fusion.32
  202.6 6.6 %multiply_convert_fusion = bf16[32,128,512]{2,1,0:T(8,128)(2,1)S(1)} fusion(f32[32,128,512]{2,1,0:T(8,128)} %get-tuple-element.30, bf16[32,128,256]{2,0,1:T(8,128)(2,1)S(1)} %slice.98, bf16[512,256]{1,0:T(8,128)(2,1)S(1)} %copy-done.15), kind=kOutput, calls=%fused_computation.1 | convolution fusion | flops 1092616192 | bytes 14942208 | tf_op jit(solution)/shard_map/lmc,hc->lmh/dot_general | solution.py:141
  209.2 1.9 copy-done.24
  211.2 3.7 fusion.29
  214.8 0.0 all-reduce.5.cloned.1.call-update
  214.8 0.3 all-reduce.7.cloned.1.call-start
  215.2 7.2 %multiply_reduce_fusion = (f32[256]{0:T(256)S(1)}, f32[32,128]{0,1:T(8,128)S(1)}, f32[32,128,256]{2,0,1:T(8,128)S(1)}) fusion(f32[32,128,256]{2,0,1:T(8,128)} %copy-done.4, f32[32,128]{0,1:T(8,128)S(1)} %add_rsqrt_fusion, f32[256]{0:T(256)S(1)} %copy-done.18, bf16[256,512]{1,0:T(8,128)(2,1)S(1)} %copy-done.23, bf16[32,128,512]{2,1,0:T(8,128)(2,1)} %copy-done.24), kind=kOutput, calls=%fused_computation.22 | convolution fusion | flops 1080028928 | bytes 12879872 | tf_op jit(solution)/shard_map/lmh,ch->lmc/dot_general | solution.py:144
  222.4 1.6 multiply_convert_fusion.2
  224.1 112.7 %all-reduce.5.cloned.1.call-done = (f32[256,512]{1,0:T(8,128)}, f32[512,256]{1,0:T(8,128)}, f32[256,128]{1,0:T(8,128)}) async-done(((f32[256,512]{1,0:T(8,128)}, f32[512,256]{1,0:T(8,128)}, f32[256,128]{1,0:T(8,128)}), (f32[256,512]{1,0:T(8,128)}, f32[512,256]{1,0:T(8,128)}, f32[256,128]{1,0:T(8,128)})) %all-reduce.5.cloned.1.call-update) | async-done | bytes 1179664 | tf_op jit(solution)/shard_map/psum | solution.py:156
  336.8 0.0 all-reduce.7.cloned.1.call-update
  336.8 0.1 collective-permute-start.2
  336.9 1.0 collective-permute-start.3
  337.9 30.7 %psum.60 = f32[256]{0:T(256)S(1)} all-reduce(f32[256]{0:T(256)S(1)} %get-tuple-element.15), channel_id=1, replica_groups=mesh['band'=8,'lon'=16] {'lon'}, use_global_device_ids=true, to_apply=%region_7.8 | all-reduce | flops 256 | bytes 2048 | tf_op jit(solution)/shard_map/psum | solution.py:156
  368.6 20.1 %psum.61 = f32[256]{0:T(256)S(1)} all-reduce(f32[256]{0:T(256)S(1)} %psum.60), channel_id=1, replica_groups=mesh['band'=8,'lon'=16] {'band'}, use_global_device_ids=true, to_apply=%region_8.9 | all-reduce | flops 256 | bytes 2048 | tf_op jit(solution)/shard_map/psum | solution.py:156
  388.7 0.6 broadcast_multiply_fusion.4
  389.3 0.3 maximum_convert_fusion.1
  389.6 0.0 copy-start.1
  389.7 4.9 %fusion.8 = f32[32,128,256]{2,0,1:T(8,128)S(1)} fusion(f32[32,130,256]{2,0,1:T(8,128)S(1)} %maximum_convert_fusion.1, f32[32,128,512]{2,0,1:T(8,128)} %copy-done.2), kind=kLoop, calls=%fused_computation.15 | loop fusion | flops 5242880 | bytes 25165824 | tf_op jit(solution)/shard_map/add | solution.py:153
  394.6 4.4 %copy.43 = f32[32,128,256]{2,1,0:T(8,128)} copy(f32[32,128,256]{2,0,1:T(8,128)S(1)} %fusion.8) | data formatting | bytes 8388608
  399.0 25.5 %all-reduce.7.cloned.1.call-done = (f32[256,512]{1,0:T(8,128)}, f32[512,256]{1,0:T(8,128)}, f32[256,128]{1,0:T(8,128)}) async-done(((f32[256,512]{1,0:T(8,128)}, f32[512,256]{1,0:T(8,128)}, f32[256,128]{1,0:T(8,128)}), (f32[256,512]{1,0:T(8,128)}, f32[512,256]{1,0:T(8,128)}, f32[256,128]{1,0:T(8,128)})) %all-reduce.7.cloned.1.call-update) | async-done | bytes 1179664 | tf_op jit(solution)/shard_map/psum | solution.py:156
  424.5 1.9 broadcast_multiply_fusion.1
  426.4 1.6 broadcast_multiply_fusion.2
  427.9 1.9 broadcast_multiply_fusion
  (49 shorter events, 0.1 us)
Async XLA Ops:
  7.2 89.9 %copy-start = (bf16[32,128,128]{2,1,0:T(8,128)(2,1)S(1)}, bf16[32,128,128]{2,1,0:T(8,128)(2,1)}, u32[]{:S(2)}) copy-start(bf16[32,128,128]{2,1,0:T(8,128)(2,1)} %param.12) | copy-start | bytes 3145732
  7.2 5.6 %copy-start.19 = (s32[1,1,32]{2,1,0:T(1,128)S(1)}, s32[1,1,32]{2,1,0:T(1,128)}, u32[]{:S(2)}) copy-start(s32[1,1,32]{2,1,0:T(1,128)} %param.11) | copy-start | bytes 388
  10.1 3.5 collective-permute-start
  12.7 3.5 collective-permute-start.1
  16.5 0.9 copy-start.18
  17.4 6.3 %copy-start.4 = (f32[32,128,256]{2,0,1:T(8,128)}, f32[32,128,256]{2,0,1:T(8,128)S(1)}, u32[]{:S(2)}) copy-start(f32[32,128,256]{2,0,1:T(8,128)S(1)} %get-tuple-element.24) | copy-start | bytes 12582916
  17.4 1.1 copy-start.22
  18.5 5.2 %copy-start.13 = (bf16[32,128,256]{2,0,1:T(8,128)(2,1)}, bf16[32,128,256]{2,0,1:T(8,128)(2,1)S(1)}, u32[]{:S(2)}) copy-start(bf16[32,128,256]{2,0,1:T(8,128)(2,1)S(1)} %multiply_convert_fusion.5) | copy-start | bytes 6291460
  18.5 7.1 %copy-start.6 = (bf16[32,128,256]{2,1,0:T(8,128)(2,1)S(1)}, bf16[32,128,256]{2,1,0:T(8,128)(2,1)}, u32[]{:S(2)}) copy-start(bf16[32,128,256]{2,1,0:T(8,128)(2,1)} %param.10) | copy-start | bytes 6291460
  18.5 7.1 %copy-start.15 = (bf16[512,256]{1,0:T(8,128)(2,1)S(1)}, bf16[512,256]{1,0:T(8,128)(2,1)}, u32[]{:S(2)}) copy-start(bf16[512,256]{1,0:T(8,128)(2,1)} %param.18) | copy-start | bytes 786436
  23.7 1.9 copy-start.11
  34.2 6.5 %copy-start.17 = (s32[32,128]{1,0:T(8,128)S(1)}, s32[32,128]{1,0:T(8,128)}, u32[]{:S(2)}) copy-start(s32[32,128]{1,0:T(8,128)} %param.13) | copy-start | bytes 49156
  34.2 6.5 %copy-start.20 = (s32[32]{0:T(128)S(1)}, s32[32]{0:T(128)}, u32[]{:S(2)}) copy-start(s32[32]{0:T(128)} %param.14) | copy-start | bytes 388
  34.2 62.8 %all-to-all-start = ((bf16[16,2,128,512]{3,2,1,0:T(8,128)(2,1)}), bf16[16,2,128,512]{3,2,1,0:T(8,128)(2,1)}, u32[]{:S(2)}, u32[]{:S(2)}) async-start(bf16[16,2,128,512]{3,2,1,0:T(8,128)(2,1)} %bitcast.68), calls=%async_computation | async-start | bytes 8388608 | tf_op jit(solution)/shard_map/all_to_all | solution.py:112
  99.3 4.1 copy-start.16
  99.3 4.1 copy-start.21
  102.0 1.4 copy-start.7
  105.7 1.1 copy-start.9
  110.9 3.4 copy-start.3
  127.5 5.4 %copy-start.8 = (bf16[32,256,128]{1,2,0:T(8,128)(2,1)S(1)}, bf16[32,256,128]{1,2,0:T(8,128)(2,1)}, u32[]{:S(2)}) copy-start(bf16[32,256,128]{1,2,0:T(8,128)(2,1)} %copy-done.7) | copy-start | bytes 6291460
  127.5 5.4 %copy-start.10 = (bf16[4096,128]{1,0:T(8,128)(2,1)S(1)}, bf16[4096,128]{1,0:T(8,128)(2,1)}, u32[]{:S(2)}) copy-start(bf16[4096,128]{1,0:T(8,128)(2,1)} %copy-done.9) | copy-start | bytes 3145732
  127.5 60.9 %all-to-all-start.1 = ((bf16[16,2,128,512]{3,2,1,0:T(8,128)(2,1)}), bf16[16,2,128,512]{3,2,1,0:T(8,128)(2,1)}, u32[]{:S(2)}, u32[]{:S(2)}) async-start(bf16[16,2,128,512]{3,2,1,0:T(8,128)(2,1)} %pad_maximum_fusion.1), calls=%async_computation.1 | async-start | bytes 8388608 | tf_op jit(solution)/shard_map/all_to_all | solution.py:125
  132.6 204.2 %all-reduce.5.cloned.1.call-start = ((), (), s32[]{:S(2)}) async-start(), calls=%async_computation.2 | async-start | bytes 2359296 | tf_op jit(solution)/shard_map/psum | solution.py:156
  193.8 8.8 %copy-start.2 = (f32[32,128,512]{2,0,1:T(8,128)}, f32[32,128,512]{2,0,1:T(8,128)S(1)}, u32[]{:S(2)}) copy-start(f32[32,128,512]{2,0,1:T(8,128)S(1)} %fusion.3) | copy-start | bytes 25165828
  193.8 5.2 %copy-start.12 = (bf16[32,128,512]{2,1,0:T(8,128)(2,1)S(1)}, bf16[32,128,512]{2,1,0:T(8,128)(2,1)}, u32[]{:S(2)}) copy-start(bf16[32,128,512]{2,1,0:T(8,128)(2,1)} %copy-done.11) | copy-start | bytes 12582916
  202.6 8.5 %copy-start.14 = (bf16[32,128,256]{2,0,1:T(8,128)(2,1)S(1)}, bf16[32,128,256]{2,0,1:T(8,128)(2,1)}, u32[]{:S(2)}) copy-start(bf16[32,128,256]{2,0,1:T(8,128)(2,1)} %copy-done.13) | copy-start | bytes 6291460
  209.2 2.0 copy-start.24
  211.1 4.0 copy-start.23
  214.8 209.7 %all-reduce.7.cloned.1.call-start = ((), (), s32[]{:S(2)}) async-start(), calls=%async_computation.3 | async-start | bytes 2359296 | tf_op jit(solution)/shard_map/psum | solution.py:156
  215.2 7.3 %copy-start.5 = (f32[32,128,256]{2,0,1:T(8,128)S(1)}, f32[32,128,256]{2,0,1:T(8,128)}, u32[]{:S(2)}) copy-start(f32[32,128,256]{2,0,1:T(8,128)} %copy-done.4) | copy-start | bytes 12582916
  336.8 52.5 %collective-permute-start.2 = (bf16[32,1,256]{2,0,1:T(8,128)(2,1)S(1)}, bf16[32,1,256]{2,0,1:T(8,128)(2,1)S(1)}, u32[]{:S(2)}, u32[]{:S(2)}) collective-permute-start(bf16[32,1,256]{2,0,1:T(8,128)(2,1)S(1)} %get-tuple-element.25), channel_id=1, source_target_pairs={{0,1},{1,2},{2,3},{3,4},{4,5},{5,6},{6,7},{7,8},{8,9},{9,10},{10,1... | collective-permute-start | bytes 49160 | tf_op jit(solution)/shard_map/ppermute | solution.py:18
  336.9 52.4 %collective-permute-start.3 = (bf16[32,1,256]{2,0,1:T(8,128)(2,1)S(1)}, bf16[32,1,256]{2,0,1:T(8,128)(2,1)S(1)}, u32[]{:S(2)}, u32[]{:S(2)}) collective-permute-start(bf16[32,1,256]{2,0,1:T(8,128)(2,1)S(1)} %get-tuple-element.26), channel_id=1, source_target_pairs={{1,0},{2,1},{3,2},{4,3},{5,4},{6,5},{7,6},{8,7},{9,8},{10,9},{11,1... | collective-permute-start | bytes 49160 | tf_op jit(solution)/shard_map/ppermute | solution.py:20
  389.6 40.2 %copy-start.1 = (bf16[32,128,128]{2,1,0:T(8,128)(2,1)S(1)}, bf16[32,128,128]{2,1,0:T(8,128)(2,1)}, u32[]{:S(2)}) copy-start(bf16[32,128,128]{2,1,0:T(8,128)(2,1)} %param.12) | copy-start | bytes 3145732
Sparse Core Ops, SparseCore 0:
  215.0 121.7 all-reduce.4
  339.5 84.9 all-reduce.6
